TPU v7x, 512 devices: a whole 4x4x16 slice. The times are simulated.
512 devices in a mesh: grp: 16 (over y, x), tile: 32 (over z, core).
Axes of the slice: x: 4, y: 4, z: 16, core: 2. Of those that a mesh axis runs over, the one named last changes fastest.
Arguments:
- jac_point: float32 [6, 2097152], P(None, ('grp', 'tile')), may hold values from -6 to 6
- jac_cam: float32 [18, 2097152], P(None, ('grp', 'tile')), may hold values from -3 to 3
- resid: float32 [2, 2097152], P(None, ('grp', 'tile')), may hold values from -6 to 6
- point_index: int32 [2097152], P(('grp', 'tile')), may hold values from 0 to 4095, as said below
- cam_index: int32 [2097152], P(('grp', 'tile')), may hold values from 0 to 12287, as said below
Outputs:
- point_step: float32 [3, 2097152], P(None, ('grp', 'tile'))
- camera_step: float32 [9, 196608], P(None, ('grp', 'tile'))
- point_resid: float32 [3, 2097152], P(None, ('grp', 'tile'))
- camera_resid: float32 [9, 196608], P(None, ('grp', 'tile'))
Inputs may be any that keep to these rules, and one draw needn't show every extreme that they name: `point_index`: index among the points of the observation's own device; every device names point 0 and point 4096 - 1. `cam_index`: block h of a device's observations (slots h * 256 to (h + 1) * 256 - 1) names cameras of group h by their index within the group; every block names camera 0 and camera 12288 - 1.
All inputs are finite; a program needn't handle non-finite values.
Results may differ from a plain program's by a relative error of at most 0.0002.
Values sent between devices are 32-bit elements; how exact they have to be, the bound alone decides.
A program may use at most 64 MiB of HBM per device.

v0:
```python
import jax
import jax.numpy as jnp
from jax import lax
from jax.sharding import PartitionSpec as P

P_DEV = 4096
CAM_DEV = 384
ITERS = 2
damping = 1.0


def segment_rows(data, ids, count):
    return jax.vmap(lambda row: jax.ops.segment_sum(row, ids, num_segments=count))(data)


def shards(jac_point, jac_cam, resid, point_index, cam_index):
    obs_dev = jac_point.shape[1]
    cam_grp = CAM_DEV * lax.axis_size("tile")
    jp = jac_point.reshape(2, 3, obs_dev)
    jc = jac_cam.reshape(2, 9, obs_dev)
    owned_index = lax.all_to_all(cam_index, "grp", split_axis=0, concat_axis=0, tiled=True)
    point_rhs = segment_rows(-jnp.sum(jp * resid[:, None], axis=0), point_index, P_DEV)
    point_diag = segment_rows(jnp.sum(jp * jp, axis=0), point_index, P_DEV)
    grad_terms, square_terms = (
        lax.all_to_all(
            -jnp.sum(jc * resid[:, None], axis=0), "grp", split_axis=1, concat_axis=1, tiled=True
        ),
        lax.all_to_all(jnp.sum(jc * jc, axis=0), "grp", split_axis=1, concat_axis=1, tiled=True),
    )
    group_terms = segment_rows(
        jnp.concatenate([grad_terms, square_terms], axis=0), owned_index, cam_grp
    )
    camera_both = lax.psum_scatter(group_terms, "tile", scatter_dimension=1, tiled=True)
    camera_rhs, camera_diag = (camera_both[:9], camera_both[9:])

    def inner(ap, ac, bp, bc):
        return jnp.sum(ap * bp) + jnp.sum(ac * bc)

    def norm_sum(rp, rc, zp, zc):
        return lax.psum(inner(rp, rc, zp, zc), ("grp", "tile"))

    point_pre = point_diag + damping
    camera_pre = camera_diag + damping
    point_x = jnp.zeros_like(point_rhs)
    camera_x = jnp.zeros_like(camera_rhs)
    point_r, camera_r = (point_rhs, camera_rhs)
    point_z, camera_z = (point_r / point_pre, camera_r / camera_pre)
    point_dir, camera_dir = (point_z, camera_z)
    norm_now = norm_sum(point_r, camera_r, point_z, camera_z)
    for step_number in range(ITERS):
        group_cams = lax.all_gather(camera_dir, "tile", axis=1, tiled=True)
        fetched = group_cams[:, owned_index]
        point_term = jnp.sum(jp * point_dir[:, point_index][None], axis=1)
        at_obs = lax.all_to_all(fetched, "grp", split_axis=1, concat_axis=1, tiled=True)
        error = point_term + jnp.sum(jc * at_obs[None], axis=1)
        column = lax.all_to_all(
            jnp.sum(jc * error[:, None], axis=0), "grp", split_axis=1, concat_axis=1, tiled=True
        )
        camera_out = lax.psum_scatter(
            segment_rows(column, owned_index, cam_grp), "tile", scatter_dimension=1, tiled=True
        )
        point_out = segment_rows(jnp.sum(jp * error[:, None], axis=0), point_index, P_DEV)
        point_q = point_out + damping * point_dir
        camera_q = camera_out + damping * camera_dir
        curve = lax.psum(inner(point_dir, camera_dir, point_q, camera_q), ("grp", "tile"))
        alpha = norm_now / curve
        point_x = point_x + alpha * point_dir
        camera_x = camera_x + alpha * camera_dir
        point_r = point_r - alpha * point_q
        camera_r = camera_r - alpha * camera_q
        if step_number + 1 < ITERS:
            point_z, camera_z = (point_r / point_pre, camera_r / camera_pre)
            norm_next = norm_sum(point_r, camera_r, point_z, camera_z)
            ratio = norm_next / norm_now
            point_dir = point_z + ratio * point_dir
            camera_dir = camera_z + ratio * camera_dir
            norm_now = norm_next
    return (point_x, camera_x, point_r, camera_r)


def solution(mesh):
    placed = (
        P(None, ("grp", "tile")),
        P(None, ("grp", "tile")),
        P(None, ("grp", "tile")),
        P(("grp", "tile")),
        P(("grp", "tile")),
    )
    return jax.shard_map(
        shards,
        mesh=mesh,
        in_specs=placed,
        out_specs=(
            P(None, ("grp", "tile")),
            P(None, ("grp", "tile")),
            P(None, ("grp", "tile")),
            P(None, ("grp", "tile")),
        ),
        check_vma=False,
    )
```

profile of v0, /device:TPU:1, one launch (start us, length us, event | category | flops | bytes accessed | tf_op | source)
XLA Modules:
  0.0 1094.1 jit_solution(12470036015440183946)
XLA Ops:
  10.1 7.6 all-to-all-start.1
  18.5 6.8 all-to-all-done.1
  25.3 3.5 all-to-all-start.2
  29.3 7.1 all-to-all-done.2
  36.4 3.5 all-to-all-start
  40.9 5.3 all-to-all-done
  46.3 25.4 %scatter_custom_fusion.2 = f32[18,12288]{0,1:T(8,128)} fusion(s32[4096]{0:T(1024)S(1)} %bitcast.80, f32[4096,18]{1,0:T(8,128)S(1)} %copy.50, f32[]{:T(128)} %constant.5.clone.1), kind=kCustom, calls=%fused_computation.15 | custom fusion | flops 73728 | bytes 884740 | tf_op jit(solution)/shard_map/vmap()/scatter-add | solution.py:13
  71.7 119.8 %reduce-scatter.4.cloned.1.call-done = f32[18,384]{0,1:T(8,128)} async-done(((f32[18,12288]{0,1:T(8,128)}), f32[18,384]{0,1:T(8,128)}) %reduce-scatter.4.cloned.1.call-update) | async-done | bytes 27664 | tf_op jit(solution)/shard_map/reduce_scatter | solution.py:33
  192.7 57.6 %all_gather.6 = f32[9,12288]{0,1:T(8,128)} all-gather(f32[9,384]{0,1:T(8,128)S(1)} %fusion.11), channel_id=1, replica_groups=mesh['grp'=16,'tile'=32] {'tile'}, dimensions={1}, use_global_device_ids=true | all-gather | bytes 456192 | tf_op jit(solution)/shard_map/all_gather | solution.py:51
  250.3 13.6 %gather_fusion.1 = f32[4096,9]{1,0:T(8,128)S(1)} fusion(f32[9,12288]{0,1:T(8,128)} %all_gather.6, s32[4096]{0:T(1024)S(1)} %broadcast_clamp_fusion), kind=kCustom, calls=%fused_computation.1 | custom fusion | bytes 311296 | tf_op jit(solution)/shard_map/gather | solution.py:52
  265.2 6.4 all-to-all-start.3
  272.3 23.8 %scatter_custom_fusion = f32[3,4096]{0,1:T(8,128)} fusion(s32[4096]{0:T(1024)S(1)} %copy-done.5, f32[4096,3]{1,0:T(8,128)S(1)} %copy.43, f32[]{:T(128)} %constant.5.clone.1), kind=kCustom, calls=%fused_computation.27 | custom fusion | flops 12288 | bytes 49156 | tf_op jit(solution)/shard_map/vmap()/scatter-add | solution.py:13
  296.8 23.7 %scatter_custom_fusion.1 = f32[3,4096]{0,1:T(8,128)} fusion(s32[4096]{0:T(1024)S(1)} %copy-done.5, f32[4096,3]{1,0:T(8,128)S(1)} %copy.44, f32[]{:T(128)} %constant.6.clone.1), kind=kCustom, calls=%fused_computation.25 | custom fusion | flops 12288 | bytes 49156 | tf_op jit(solution)/shard_map/vmap()/scatter-add | solution.py:13
  323.0 14.2 %gather_fusion = f32[4096,3]{1,0:T(8,128)} fusion(f32[3,4096]{0,1:T(8,128)S(1)} %div.21, s32[4096]{0:T(1024)S(1)} %fusion.12), kind=kCustom, calls=%fused_computation | custom fusion | bytes 114688 | tf_op jit(solution)/shard_map/gather | solution.py:53
  340.3 14.0 %all_to_all.72 = f32[9,16,256]{2,0,1:T(8,128)S(1)} all-to-all(f32[9,16,256]{2,0,1:T(8,128)S(1)} %copy.55), channel_id=1, replica_groups=mesh['grp'=16,'tile'=32] {'grp'}, dimensions={1} | all-to-all | bytes 294912 | tf_op jit(solution)/shard_map/all_to_all | solution.py:56
  356.5 25.7 %scatter_custom_fusion.4 = f32[9,12288]{0,1:T(8,128)} fusion(s32[4096]{0:T(1024)S(1)} %bitcast.82, f32[4096,9]{1,0:T(8,128)} %copy.57, f32[]{:T(128)} %constant.5.clone.1), kind=kCustom, calls=%fused_computation.13 | custom fusion | flops 36864 | bytes 442880 | tf_op jit(solution)/shard_map/vmap()/scatter-add | solution.py:13
  384.3 23.4 %scatter_fusion = f32[3,4096]{0,1:T(8,128)S(1)} fusion(f32[3,4096]{0,1:T(8,128)S(1)} %copy-done.2, s32[4096]{0:T(1024)S(1)} %copy-done.5, f32[4096,3]{1,0:T(8,128)} %copy.54), kind=kCustom, calls=%fused_computation.7 | custom fusion | flops 12288 | bytes 163840 | tf_op jit(solution)/shard_map/vmap()/scatter-add | solution.py:13
  407.8 3.5 multiply_reduce_fusion.2
  411.2 82.1 %reduce-scatter.6.cloned.1.call-done = f32[9,384]{0,1:T(8,128)} async-done(((f32[9,12288]{0,1:T(8,128)}), f32[9,384]{0,1:T(8,128)}) %reduce-scatter.6.cloned.1.call-update) | async-done | bytes 13840 | tf_op jit(solution)/shard_map/reduce_scatter | solution.py:59
  497.6 106.2 %all-reduce = (f32[]{:T(128)}, f32[]{:T(128)}) all-reduce(f32[]{:T(128)S(6)} %add.103, f32[]{:T(128)S(6)} %add.108), channel_id=1, replica_groups=mesh['grp'=16,'tile'=32] {'grp','tile'}, use_global_device_ids=true, to_apply=%region_10.0 | all-reduce | flops 2 | bytes 16 | tf_op jit(solution)/shard_map/psum | solution.py:40
  605.1 5.3 multiply_reduce_fusion.1
  612.4 98.4 %psum.30 = f32[]{:T(128)} all-reduce(f32[]{:T(128)S(6)} %add.109), channel_id=1, replica_groups=mesh['grp'=16,'tile'=32] {'grp','tile'}, use_global_device_ids=true, to_apply=%region_23.0 | all-reduce | flops 1 | bytes 8 | tf_op jit(solution)/shard_map/psum | solution.py:40
  712.3 53.8 %all_gather.7 = f32[9,12288]{0,1:T(8,128)} all-gather(f32[9,384]{0,1:T(8,128)S(1)} %multiply_add_fusion.3), channel_id=1, replica_groups=mesh['grp'=16,'tile'=32] {'tile'}, dimensions={1}, use_global_device_ids=true | all-gather | bytes 456192 | tf_op jit(solution)/shard_map/all_gather | solution.py:51
  766.2 17.0 %gather_fusion.3 = f32[4096,9]{1,0:T(8,128)} fusion(f32[9,12288]{0,1:T(8,128)} %all_gather.7, s32[4096]{0:T(1024)S(1)} %broadcast_clamp_fusion), kind=kCustom, calls=%fused_computation.3 | custom fusion | bytes 311296 | tf_op jit(solution)/shard_map/gather | solution.py:52
  786.1 4.2 all-to-all-start.5
  793.7 15.7 %gather_fusion.2 = f32[4096,3]{1,0:T(8,128)} fusion(f32[3,4096]{0,1:T(8,128)} %multiply_add_fusion.1, s32[4096]{0:T(1024)S(1)} %fusion.12), kind=kCustom, calls=%fused_computation.2 | custom fusion | bytes 114688 | tf_op jit(solution)/shard_map/gather | solution.py:53
  813.4 14.4 %all_to_all.73 = f32[9,16,256]{2,0,1:T(8,128)S(1)} all-to-all(f32[9,16,256]{2,0,1:T(8,128)S(1)} %copy.62), channel_id=1, replica_groups=mesh['grp'=16,'tile'=32] {'grp'}, dimensions={1} | all-to-all | bytes 294912 | tf_op jit(solution)/shard_map/all_to_all | solution.py:56
  830.0 25.7 %scatter_custom_fusion.6 = f32[9,12288]{0,1:T(8,128)} fusion(s32[4096]{0:T(1024)S(1)} %bitcast.83, f32[4096,9]{1,0:T(8,128)} %copy.64, f32[]{:T(128)} %constant.5.clone.1), kind=kCustom, calls=%fused_computation.11 | custom fusion | flops 36864 | bytes 442880 | tf_op jit(solution)/shard_map/vmap()/scatter-add | solution.py:13
  860.8 23.3 %scatter_fusion.1 = f32[3,4096]{0,1:T(8,128)} fusion(f32[3,4096]{0,1:T(8,128)} %copy.80, s32[4096]{0:T(1024)S(1)} %copy-done.5, f32[4096,3]{1,0:T(8,128)} %copy.61), kind=kCustom, calls=%fused_computation.9 | custom fusion | flops 12288 | bytes 163840 | tf_op jit(solution)/shard_map/vmap()/scatter-add | solution.py:13
  887.4 78.7 %reduce-scatter.8.cloned.1.call-done = f32[9,384]{0,1:T(8,128)} async-done(((f32[9,12288]{0,1:T(8,128)}), f32[9,384]{0,1:T(8,128)}) %reduce-scatter.8.cloned.1.call-update) | async-done | bytes 13840 | tf_op jit(solution)/shard_map/reduce_scatter | solution.py:59
  969.0 106.2 %psum.31 = f32[]{:T(128)} all-reduce(f32[]{:T(128)S(6)} %add.114), channel_id=1, replica_groups=mesh['grp'=16,'tile'=32] {'grp','tile'}, use_global_device_ids=true, to_apply=%region_33.0 | all-reduce | flops 1 | bytes 8 | tf_op jit(solution)/shard_map/psum | solution.py:65
  1078.1 5.3 multiply_subtract_fusion
  (99 shorter events, 49.7 us)
Async XLA Ops:
  9.1 19.8 %copy-start.7 = (f32[6,4096]{1,0:T(8,128)S(1)}, f32[6,4096]{1,0:T(8,128)}, u32[]{:S(2)}) copy-start(f32[6,4096]{1,0:T(8,128)} %param.5) | copy-start | bytes 294916
  9.1 19.8 %copy-start.6 = (f32[2,4096]{1,0:T(2,128)S(1)}, f32[2,4096]{1,0:T(2,128)}, u32[]{:S(2)}) copy-start(f32[2,4096]{1,0:T(2,128)} %param.7) | copy-start | bytes 98308
  10.1 15.3 %all-to-all-start.1 = ((f32[9,16,256]{2,0,1:T(8,128)}), f32[9,16,256]{2,0,1:T(8,128)S(1)}, u32[]{:S(2)}, u32[]{:S(2)}) async-start(f32[9,16,256]{2,0,1:T(8,128)} %copy.46), calls=%async_computation.1 | async-start | bytes 524288 | tf_op jit(solution)/shard_map/all_to_all | solution.py:25
  25.3 11.0 %all-to-all-start.2 = ((f32[9,16,256]{2,0,1:T(8,128)}), f32[9,16,256]{2,0,1:T(8,128)S(1)}, u32[]{:S(2)}, u32[]{:S(2)}) async-start(f32[9,16,256]{2,0,1:T(8,128)} %copy.48), calls=%async_computation.2 | async-start | bytes 524288 | tf_op jit(solution)/shard_map/all_to_all | solution.py:28
  36.4 9.9 all-to-all-start
  39.9 151.6 %reduce-scatter.4.cloned.1.call-start = ((), (), s32[]{:S(2)}) async-start(), calls=%async_computation.10 | async-start | bytes 6488064 | tf_op jit(solution)/shard_map/reduce_scatter | solution.py:33
  250.2 21.4 %copy-start.5 = (s32[4096]{0:T(1024)S(1)}, s32[4096]{0:T(1024)}, u32[]{:S(2)}) copy-start(s32[4096]{0:T(1024)} %param.8) | copy-start | bytes 49156
  265.2 74.4 %all-to-all-start.3 = ((f32[9,16,256]{2,0,1:T(8,128)}), f32[9,16,256]{2,0,1:T(8,128)S(1)}, u32[]{:S(2)}, u32[]{:S(2)}) async-start(f32[9,16,256]{2,0,1:T(8,128)} %copy.52), calls=%async_computation.4 | async-start | bytes 524288 | tf_op jit(solution)/shard_map/all_to_all | solution.py:54
  271.6 221.7 %reduce-scatter.6.cloned.1.call-start = ((), (), s32[]{:S(2)}) async-start(), calls=%async_computation.11 | async-start | bytes 6488064 | tf_op jit(solution)/shard_map/reduce_scatter | solution.py:59
  323.0 59.2 %copy-start = (f32[3,4096]{0,1:T(8,128)}, f32[3,4096]{0,1:T(8,128)S(1)}, u32[]{:S(2)}) copy-start(f32[3,4096]{0,1:T(8,128)S(1)} %div.21) | copy-start | bytes 147460
  382.3 2.1 copy-start.2
  407.8 85.6 %copy-start.3 = (f32[18,384]{0,1:T(8,128)S(1)}, f32[18,384]{0,1:T(8,128)}, u32[]{:S(2)}) copy-start(f32[18,384]{0,1:T(8,128)} %reduce-scatter.4.cloned.1.call-done) | copy-start | bytes 82948
  766.2 24.4 %copy-start.1 = (f32[3,4096]{0,1:T(8,128)S(1)}, f32[3,4096]{0,1:T(8,128)}, u32[]{:S(2)}) copy-start(f32[3,4096]{0,1:T(8,128)} %copy-done) | copy-start | bytes 147460
  786.1 25.6 %all-to-all-start.5 = ((f32[9,16,256]{2,0,1:T(8,128)}), f32[9,16,256]{2,0,1:T(8,128)}, u32[]{:S(2)}, u32[]{:S(2)}) async-start(f32[9,16,256]{2,0,1:T(8,128)} %copy.59), calls=%async_computation.7 | async-start | bytes 524288 | tf_op jit(solution)/shard_map/all_to_all | solution.py:54
  790.3 175.8 %reduce-scatter.8.cloned.1.call-start = ((), (), s32[]{:S(2)}) async-start(), calls=%async_computation.12 | async-start | bytes 6488064 | tf_op jit(solution)/shard_map/reduce_scatter | solution.py:59
  1083.3 3.0 copy-start.4
Sparse Core Ops, SparseCore 0:
  71.8 119.6 reduce-scatter.3
  382.4 110.9 reduce-scatter.5
  855.8 110.2 reduce-scatter.7
where the time goes:
time: 1100 us; the launch traced here: 1090 us
  blocking collectives  451 us (41%)
  waiting for transfers between devices  300 us (27%)
  other arithmetic  201 us (18%)
  local copies, waits for them, and re-layouts  93.5 us (8%)
  starting transfers between devices  25.5 us (2%)
  between operations  23.5 us (2%)
    psum x2, blocking collectives, norm_sum(): return lax.psum(inner(rp, rc, zp, zc), ('grp', 'tile'))  205 us
    scatter-add x7, other arithmetic, segment_rows(): jax.ops.segment_sum(row, ids, num_segments=count)  171 us
    reduce_scatter x2, waiting for transfers between devices, shards(): lax.psum_scatter(segment_rows(column, owned_index, cam_grp), 'tile', scat...  161 us
    reduce_scatter x1, waiting for transfers between devices, shards(): lax.psum_scatter(group_terms, 'tile', scatter_dimension=1, tiled=True)  120 us
    all_gather x2, blocking collectives, shards(): group_cams = lax.all_gather(camera_dir, 'tile', axis=1, tiled=True)  111 us
    psum x1, blocking collectives, shards(): lax.psum(inner(point_dir, camera_dir, point_q, camera_q), ('grp', 'tile'))  106 us
    gather x4, local copies, waits for them, and re-layouts, shards(): point_term = jnp.sum(jp * point_dir[:, point_index][None], axis=1)  34.3 us
    gather x2, local copies, waits for them, and re-layouts, shards(): fetched = group_cams[:, owned_index]  30.6 us
  transfers between devices with their start and end apart: 8, of which 6 were waited for; matrix products, arithmetic and copies ran while one was open for 14% of the time, Pallas kernels for 0%

commit v1 on v0

--- a/solution.py
+++ b/solution.py
@@ -7,6 +7,14 @@
 CAM_DEV = 384
 ITERS = 2
 damping = 1.0
+
+
+def _set_pipes(xx):
+    chip_axis = "tile"
+    dev_axis = "grp"
+    for hop_no in (dev_axis, chip_axis):
+        xx = lax.psum(xx, axis_name=hop_no)
+    return xx
 
 
 def segment_rows(data, ids, count):
@@ -37,7 +45,7 @@
         return jnp.sum(ap * bp) + jnp.sum(ac * bc)
 
     def norm_sum(rp, rc, zp, zc):
-        return lax.psum(inner(rp, rc, zp, zc), ("grp", "tile"))
+        return _set_pipes(inner(rp, rc, zp, zc))
 
     point_pre = point_diag + damping
     camera_pre = camera_diag + damping

time: 1100 us -> 1160 us (1.055)
  blocking collectives: 451 us -> 519 us
    psum x1 -> x2, blocking collectives: 106 us -> 205 us  [shards(): lax.psum(inner(point_dir, camera_dir, point_q, camera_q), ('grp', 'tile'))]
    psum x2 -> x4, blocking collectives: 205 us -> 175 us  [_set_pipes(): xx = lax.psum(xx, axis_name=hop_no)]
  transfers between devices with their start and end apart: 8 -> 8, of which waited for: 6 -> 6; matrix products, arithmetic and copies ran while one was open for 14% -> 13% of each run, Pallas kernels for 0% -> 0%
where the time goes in v1:
time: 1160 us
  blocking collectives  519 us (45%)
  waiting for transfers between devices  299 us (26%)
  other arithmetic  201 us (17%)
  local copies, waits for them, and re-layouts  93.5 us (8%)
  starting transfers between devices  25.5 us (2%)
  between operations  23.5 us (2%)
    psum x2, blocking collectives, shards(): lax.psum(inner(point_dir, camera_dir, point_q, camera_q), ('grp', 'tile'))  205 us
    psum x4, blocking collectives, _set_pipes(): xx = lax.psum(xx, axis_name=hop_no)  175 us
    scatter-add x7, other arithmetic, segment_rows(): jax.ops.segment_sum(row, ids, num_segments=count)  171 us
    reduce_scatter x2, waiting for transfers between devices, shards(): lax.psum_scatter(segment_rows(column, owned_index, cam_grp), 'tile', scat...  160 us
    reduce_scatter x1, waiting for transfers between devices, shards(): lax.psum_scatter(group_terms, 'tile', scatter_dimension=1, tiled=True)  120 us
    all_gather x2, blocking collectives, shards(): group_cams = lax.all_gather(camera_dir, 'tile', axis=1, tiled=True)  112 us
    gather x4, local copies, waits for them, and re-layouts, shards(): point_term = jnp.sum(jp * point_dir[:, point_index][None], axis=1)  34.3 us
    gather x2, local copies, waits for them, and re-layouts, shards(): fetched = group_cams[:, owned_index]  30.6 us
  transfers between devices with their start and end apart: 8, of which 6 were waited for; matrix products, arithmetic and copies ran while one was open for 13% of the time, Pallas kernels for 0%

profile of v1, /device:TPU:1, one launch (start us, length us, event | category | flops | bytes accessed | tf_op | source)
XLA Modules:
  0.0 1162.2 jit_solution(4338356085256454863)
XLA Ops:
  10.1 7.6 all-to-all-start.1
  18.5 6.8 all-to-all-done.1
  29.3 7.1 all-to-all-done.2
  40.9 5.3 all-to-all-done
  46.3 25.4 %scatter_custom_fusion.2 = f32[18,12288]{0,1:T(8,128)} fusion(s32[4096]{0:T(1024)S(1)} %bitcast.80, f32[4096,18]{1,0:T(8,128)S(1)} %copy.50, f32[]{:T(128)} %constant.5.clone.1), kind=kCustom, calls=%fused_computation.15 | custom fusion | flops 73728 | bytes 884740 | tf_op jit(solution)/shard_map/vmap()/scatter-add | solution.py:21
  71.7 119.8 %reduce-scatter.4.cloned.1.call-done = f32[18,384]{0,1:T(8,128)} async-done(((f32[18,12288]{0,1:T(8,128)}), f32[18,384]{0,1:T(8,128)}) %reduce-scatter.4.cloned.1.call-update) | async-done | bytes 27664 | tf_op jit(solution)/shard_map/reduce_scatter | solution.py:41
  192.7 57.6 %all_gather.6 = f32[9,12288]{0,1:T(8,128)} all-gather(f32[9,384]{0,1:T(8,128)S(1)} %fusion.11), channel_id=1, replica_groups=mesh['grp'=16,'tile'=32] {'tile'}, dimensions={1}, use_global_device_ids=true | all-gather | bytes 456192 | tf_op jit(solution)/shard_map/all_gather | solution.py:59
  250.3 13.6 %gather_fusion.1 = f32[4096,9]{1,0:T(8,128)S(1)} fusion(f32[9,12288]{0,1:T(8,128)} %all_gather.6, s32[4096]{0:T(1024)S(1)} %broadcast_clamp_fusion), kind=kCustom, calls=%fused_computation.1 | custom fusion | bytes 311296 | tf_op jit(solution)/shard_map/gather | solution.py:60
  265.2 6.4 all-to-all-start.3
  272.3 23.8 %scatter_custom_fusion = f32[3,4096]{0,1:T(8,128)} fusion(s32[4096]{0:T(1024)S(1)} %copy-done.5, f32[4096,3]{1,0:T(8,128)S(1)} %copy.43, f32[]{:T(128)} %constant.5.clone.1), kind=kCustom, calls=%fused_computation.27 | custom fusion | flops 12288 | bytes 49156 | tf_op jit(solution)/shard_map/vmap()/scatter-add | solution.py:21
  296.8 23.7 %scatter_custom_fusion.1 = f32[3,4096]{0,1:T(8,128)} fusion(s32[4096]{0:T(1024)S(1)} %copy-done.5, f32[4096,3]{1,0:T(8,128)S(1)} %copy.44, f32[]{:T(128)} %constant.6.clone.1), kind=kCustom, calls=%fused_computation.25 | custom fusion | flops 12288 | bytes 49156 | tf_op jit(solution)/shard_map/vmap()/scatter-add | solution.py:21
  323.0 14.2 %gather_fusion = f32[4096,3]{1,0:T(8,128)} fusion(f32[3,4096]{0,1:T(8,128)S(1)} %div.21, s32[4096]{0:T(1024)S(1)} %fusion.12), kind=kCustom, calls=%fused_computation | custom fusion | bytes 114688 | tf_op jit(solution)/shard_map/gather | solution.py:61
  340.3 14.0 %all_to_all.72 = f32[9,16,256]{2,0,1:T(8,128)S(1)} all-to-all(f32[9,16,256]{2,0,1:T(8,128)S(1)} %copy.55), channel_id=1, replica_groups=mesh['grp'=16,'tile'=32] {'grp'}, dimensions={1} | all-to-all | bytes 294912 | tf_op jit(solution)/shard_map/all_to_all | solution.py:64
  356.5 25.7 %scatter_custom_fusion.4 = f32[9,12288]{0,1:T(8,128)} fusion(s32[4096]{0:T(1024)S(1)} %bitcast.82, f32[4096,9]{1,0:T(8,128)} %copy.57, f32[]{:T(128)} %constant.5.clone.1), kind=kCustom, calls=%fused_computation.13 | custom fusion | flops 36864 | bytes 442880 | tf_op jit(solution)/shard_map/vmap()/scatter-add | solution.py:21
  384.3 23.4 %scatter_fusion = f32[3,4096]{0,1:T(8,128)S(1)} fusion(f32[3,4096]{0,1:T(8,128)S(1)} %copy-done.2, s32[4096]{0:T(1024)S(1)} %copy-done.5, f32[4096,3]{1,0:T(8,128)} %copy.54), kind=kCustom, calls=%fused_computation.7 | custom fusion | flops 12288 | bytes 163840 | tf_op jit(solution)/shard_map/vmap()/scatter-add | solution.py:21
  411.2 82.1 %reduce-scatter.6.cloned.1.call-done = f32[9,384]{0,1:T(8,128)} async-done(((f32[9,12288]{0,1:T(8,128)}), f32[9,384]{0,1:T(8,128)}) %reduce-scatter.6.cloned.1.call-update) | async-done | bytes 13840 | tf_op jit(solution)/shard_map/reduce_scatter | solution.py:67
  496.3 33.9 %psum.42 = f32[]{:T(128)} all-reduce(f32[]{:T(128)S(6)} %add.107), channel_id=1, replica_groups=mesh['grp'=16,'tile'=32] {'grp'}, use_global_device_ids=true, to_apply=%region_10.0 | all-reduce | flops 1 | bytes 8 | tf_op jit(solution)/shard_map/psum | solution.py:16
  531.5 56.4 %psum.43 = f32[]{:T(128)} all-reduce(f32[]{:T(128)} %psum.42), channel_id=1, replica_groups=mesh['grp'=16,'tile'=32] {'tile'}, use_global_device_ids=true, to_apply=%region_11.0 | all-reduce | flops 1 | bytes 8 | tf_op jit(solution)/shard_map/psum | solution.py:16
  587.9 98.8 %psum.44 = f32[]{:T(128)} all-reduce(f32[]{:T(128)S(6)} %add.112), channel_id=1, replica_groups=mesh['grp'=16,'tile'=32] {'grp','tile'}, use_global_device_ids=true, to_apply=%region_21.0 | all-reduce | flops 1 | bytes 8 | tf_op jit(solution)/shard_map/psum | solution.py:73
  688.1 5.3 multiply_reduce_fusion.1
  695.4 30.3 %psum.45 = f32[]{:T(128)} all-reduce(f32[]{:T(128)S(6)} %add.113), channel_id=1, replica_groups=mesh['grp'=16,'tile'=32] {'grp'}, use_global_device_ids=true, to_apply=%region_24.0 | all-reduce | flops 1 | bytes 8 | tf_op jit(solution)/shard_map/psum | solution.py:16
  725.7 54.0 %psum.46 = f32[]{:T(128)} all-reduce(f32[]{:T(128)} %psum.45), channel_id=1, replica_groups=mesh['grp'=16,'tile'=32] {'tile'}, use_global_device_ids=true, to_apply=%region_25.0 | all-reduce | flops 1 | bytes 8 | tf_op jit(solution)/shard_map/psum | solution.py:16
  781.1 53.9 %all_gather.7 = f32[9,12288]{0,1:T(8,128)} all-gather(f32[9,384]{0,1:T(8,128)S(1)} %multiply_add_fusion.3), channel_id=1, replica_groups=mesh['grp'=16,'tile'=32] {'tile'}, dimensions={1}, use_global_device_ids=true | all-gather | bytes 456192 | tf_op jit(solution)/shard_map/all_gather | solution.py:59
  835.0 17.0 %gather_fusion.3 = f32[4096,9]{1,0:T(8,128)} fusion(f32[9,12288]{0,1:T(8,128)} %all_gather.7, s32[4096]{0:T(1024)S(1)} %broadcast_clamp_fusion), kind=kCustom, calls=%fused_computation.3 | custom fusion | bytes 311296 | tf_op jit(solution)/shard_map/gather | solution.py:60
  854.9 4.2 all-to-all-start.5
  862.6 15.7 %gather_fusion.2 = f32[4096,3]{1,0:T(8,128)} fusion(f32[3,4096]{0,1:T(8,128)} %multiply_add_fusion.1, s32[4096]{0:T(1024)S(1)} %fusion.12), kind=kCustom, calls=%fused_computation.2 | custom fusion | bytes 114688 | tf_op jit(solution)/shard_map/gather | solution.py:61
  882.2 14.4 %all_to_all.73 = f32[9,16,256]{2,0,1:T(8,128)S(1)} all-to-all(f32[9,16,256]{2,0,1:T(8,128)S(1)} %copy.62), channel_id=1, replica_groups=mesh['grp'=16,'tile'=32] {'grp'}, dimensions={1} | all-to-all | bytes 294912 | tf_op jit(solution)/shard_map/all_to_all | solution.py:64
  898.9 25.7 %scatter_custom_fusion.6 = f32[9,12288]{0,1:T(8,128)} fusion(s32[4096]{0:T(1024)S(1)} %bitcast.83, f32[4096,9]{1,0:T(8,128)} %copy.64, f32[]{:T(128)} %constant.5.clone.1), kind=kCustom, calls=%fused_computation.11 | custom fusion | flops 36864 | bytes 442880 | tf_op jit(solution)/shard_map/vmap()/scatter-add | solution.py:21
  929.6 23.3 %scatter_fusion.1 = f32[3,4096]{0,1:T(8,128)} fusion(f32[3,4096]{0,1:T(8,128)} %copy.80, s32[4096]{0:T(1024)S(1)} %copy-done.5, f32[4096,3]{1,0:T(8,128)} %copy.61), kind=kCustom, calls=%fused_computation.9 | custom fusion | flops 12288 | bytes 163840 | tf_op jit(solution)/shard_map/vmap()/scatter-add | solution.py:21
  956.3 78.0 %reduce-scatter.8.cloned.1.call-done = f32[9,384]{0,1:T(8,128)} async-done(((f32[9,12288]{0,1:T(8,128)}), f32[9,384]{0,1:T(8,128)}) %reduce-scatter.8.cloned.1.call-update) | async-done | bytes 13840 | tf_op jit(solution)/shard_map/reduce_scatter | solution.py:67
  1037.2 106.1 %psum.47 = f32[]{:T(128)} all-reduce(f32[]{:T(128)S(6)} %add.118), channel_id=1, replica_groups=mesh['grp'=16,'tile'=32] {'grp','tile'}, use_global_device_ids=true, to_apply=%region_35.0 | all-reduce | flops 1 | bytes 8 | tf_op jit(solution)/shard_map/psum | solution.py:73
  1146.2 5.3 multiply_subtract_fusion
  (102 shorter events, 60.2 us)
Async XLA Ops:
  9.1 19.8 %copy-start.7 = (f32[6,4096]{1,0:T(8,128)S(1)}, f32[6,4096]{1,0:T(8,128)}, u32[]{:S(2)}) copy-start(f32[6,4096]{1,0:T(8,128)} %param.5) | copy-start | bytes 294916
  9.1 19.8 %copy-start.6 = (f32[2,4096]{1,0:T(2,128)S(1)}, f32[2,4096]{1,0:T(2,128)}, u32[]{:S(2)}) copy-start(f32[2,4096]{1,0:T(2,128)} %param.7) | copy-start | bytes 98308
  10.1 15.3 %all-to-all-start.1 = ((f32[9,16,256]{2,0,1:T(8,128)}), f32[9,16,256]{2,0,1:T(8,128)S(1)}, u32[]{:S(2)}, u32[]{:S(2)}) async-start(f32[9,16,256]{2,0,1:T(8,128)} %copy.46), calls=%async_computation.1 | async-start | bytes 524288 | tf_op jit(solution)/shard_map/all_to_all | solution.py:33
  25.3 11.0 all-to-all-start.2
  36.4 9.9 all-to-all-start
  39.9 151.6 %reduce-scatter.4.cloned.1.call-start = ((), (), s32[]{:S(2)}) async-start(), calls=%async_computation.10 | async-start | bytes 6488064 | tf_op jit(solution)/shard_map/reduce_scatter | solution.py:41
  250.2 21.4 %copy-start.5 = (s32[4096]{0:T(1024)S(1)}, s32[4096]{0:T(1024)}, u32[]{:S(2)}) copy-start(s32[4096]{0:T(1024)} %param.8) | copy-start | bytes 49156
  265.2 74.4 %all-to-all-start.3 = ((f32[9,16,256]{2,0,1:T(8,128)}), f32[9,16,256]{2,0,1:T(8,128)S(1)}, u32[]{:S(2)}, u32[]{:S(2)}) async-start(f32[9,16,256]{2,0,1:T(8,128)} %copy.52), calls=%async_computation.4 | async-start | bytes 524288 | tf_op jit(solution)/shard_map/all_to_all | solution.py:62
  271.6 221.7 %reduce-scatter.6.cloned.1.call-start = ((), (), s32[]{:S(2)}) async-start(), calls=%async_computation.11 | async-start | bytes 6488064 | tf_op jit(solution)/shard_map/reduce_scatter | solution.py:67
  323.0 59.2 %copy-start = (f32[3,4096]{0,1:T(8,128)}, f32[3,4096]{0,1:T(8,128)S(1)}, u32[]{:S(2)}) copy-start(f32[3,4096]{0,1:T(8,128)S(1)} %div.21) | copy-start | bytes 147460
  382.3 2.1 copy-start.2
  407.8 85.6 %copy-start.3 = (f32[18,384]{0,1:T(8,128)S(1)}, f32[18,384]{0,1:T(8,128)}, u32[]{:S(2)}) copy-start(f32[18,384]{0,1:T(8,128)} %reduce-scatter.4.cloned.1.call-done) | copy-start | bytes 82948
  835.0 24.4 %copy-start.1 = (f32[3,4096]{0,1:T(8,128)S(1)}, f32[3,4096]{0,1:T(8,128)}, u32[]{:S(2)}) copy-start(f32[3,4096]{0,1:T(8,128)} %copy-done) | copy-start | bytes 147460
  854.9 25.6 %all-to-all-start.5 = ((f32[9,16,256]{2,0,1:T(8,128)}), f32[9,16,256]{2,0,1:T(8,128)}, u32[]{:S(2)}, u32[]{:S(2)}) async-start(f32[9,16,256]{2,0,1:T(8,128)} %copy.59), calls=%async_computation.7 | async-start | bytes 524288 | tf_op jit(solution)/shard_map/all_to_all | solution.py:62
  859.1 175.1 %reduce-scatter.8.cloned.1.call-start = ((), (), s32[]{:S(2)}) async-start(), calls=%async_computation.12 | async-start | bytes 6488064 | tf_op jit(solution)/shard_map/reduce_scatter | solution.py:67
  1151.5 3.0 copy-start.4
Sparse Core Ops, SparseCore 0:
  71.8 119.6 reduce-scatter.3
  382.4 110.9 reduce-scatter.5
  924.7 109.5 reduce-scatter.7
